TPU v7x, 32 devices: a whole 2x2x4 slice. The times are simulated.
32 devices in a mesh: dp: 16 (over z, x, core), rows: 2 (over y).
Axes of the slice: x: 2, y: 2, z: 4, core: 2. Of those that a mesh axis runs over, the one named last changes fastest.
Arguments:
- features: bfloat16 [32, 12, 64, 1024], P('dp', 'rows'), may hold values from -8 to 8
- first_atrous_weight: bfloat16 [3, 3, 1024, 256], P(None, None, 'dp'), may hold values from -0.0625 to 0.0625
- second_atrous_weight: bfloat16 [3, 3, 1024, 256], P(None, None, 'dp'), may hold values from -0.0625 to 0.0625
- third_atrous_weight: bfloat16 [3, 3, 1024, 256], P(None, None, 'dp'), may hold values from -0.0625 to 0.0625
- pointwise_weight: bfloat16 [1024, 256], replicated, may hold values from -0.1875 to 0.1875
- pooling_weight: bfloat16 [1024, 256], replicated, may hold values from -0.1875 to 0.1875
- projection_weight: bfloat16 [1280, 256], replicated, may hold values from -0.15625 to 0.15625
- branch_norm_gain: float32 [4, 256], replicated, may hold values from 0.25 to 1.75
- branch_norm_shift: float32 [4, 256], replicated, may hold values from -3 to 3
- projection_norm_gain: float32 [256], replicated, may hold values from 0.25 to 1.75
- projection_norm_shift: float32 [256], replicated, may hold values from -3 to 3
- ghost_group_index: int32 [32], replicated, may hold values from 0 to 7, as said below
Outputs:
- decoder_in: bfloat16 [32, 12, 64, 256], P(None, 'rows', 'dp')
Inputs may be any that keep to these rules, and one draw needn't show every extreme that they name: `ghost_group_index`: each of the 8 group ids names exactly 4 images.
All inputs are finite; a program needn't handle non-finite values.
Results may differ from a plain program's by a relative error of at most 0.0014.
The roundings to bfloat16 on the way count: a program that leaves them out, or rounds other values in their place, can miss the bound.
Values may be sent and summed in bfloat16 or wider, within the bound.
No kernel may reach another device: no remote copies, remote signals or barrier semaphores. Data moves between devices by JAX's collectives and lax.ppermute only.
A program may use at most 128 MiB of HBM per device.

v0:
```python
import jax
import jax.numpy as jnp
from jax import lax
from jax.sharding import PartitionSpec as P

DILATION_FIRST = 12
DILATION_SECOND = 24
DILATION_THIRD = 36


def from_behind(array, axis, by):
    count = lax.axis_size(axis)
    pairs = [(i, i + by) for i in range(count) if 0 <= i + by < count]
    return lax.ppermute(array, axis, pairs)


def row_tap_list(block_tensor, kernel_row_slice, dilation_rate):
    partial_terms = jnp.einsum(
        "irwc,kco->irwko", block_tensor, kernel_row_slice, preferred_element_type=jnp.float32
    )
    map_width = block_tensor.shape[2]
    left_padding = jnp.pad(partial_terms[:, :, :, 0], ((0, 0), (0, 0), (dilation_rate, 0), (0, 0)))[
        :, :, :map_width
    ]
    right_padding = jnp.pad(
        partial_terms[:, :, :, 2], ((0, 0), (0, 0), (0, dilation_rate), (0, 0))
    )[:, :, dilation_rate:]
    return partial_terms[:, :, :, 1] + left_padding + right_padding


def dilated_result(features, kernel_weight, dilation_rate):
    step_offsets = dilation_rate // features.shape[1]
    running_sum = row_tap_list(features, kernel_weight[1], dilation_rate)
    for by_dev, tap_offset in ((step_offsets, 0), (-step_offsets, 2)):
        partial_taps = row_tap_list(features, kernel_weight[tap_offset], dilation_rate)
        running_sum = running_sum + from_behind(partial_taps, "rows", by_dev)
    return running_sum


def stats_terms(pre, onehot):
    first = jnp.sum(pre, axis=(1, 2))
    second = jnp.sum(pre * pre, axis=(1, 2))
    group_first = jnp.dot(onehot.T, first, precision=lax.Precision.HIGHEST)
    group_second = jnp.dot(onehot.T, second, precision=lax.Precision.HIGHEST)
    return (group_first, group_second)


def apply_norm(pre, onehot, total_first, total_second, count, gain, shift):
    mean = total_first / count
    var = total_second / count - mean * mean
    inv = lax.rsqrt(var + 1e-05)
    img_mean = jnp.dot(onehot, mean, precision=lax.Precision.HIGHEST)
    img_inv = jnp.dot(onehot, inv, precision=lax.Precision.HIGHEST)
    scaled = (pre - img_mean[:, None, None, :]) * img_inv[:, None, None, :] * gain + shift
    return jax.nn.relu(scaled).astype(jnp.bfloat16)


def project(joined, onehot, projection_weight, count, projection_norm_gain, projection_norm_shift):
    proj = jnp.einsum(
        "irwc,co->irwo", joined, projection_weight, preferred_element_type=jnp.float32
    )
    group_first, group_second = stats_terms(proj, onehot)
    total_first, total_second = lax.psum((group_first, group_second), ("dp", "rows"))
    return apply_norm(
        proj, onehot, total_first, total_second, count, projection_norm_gain, projection_norm_shift
    )


def shards(
    features,
    first_atrous_weight,
    second_atrous_weight,
    third_atrous_weight,
    pointwise_weight,
    pooling_weight,
    projection_weight,
    branch_norm_gain,
    branch_norm_shift,
    projection_norm_gain,
    projection_norm_shift,
    ghost_group_index,
):
    img_dev, rows_dev, cols, chans = features.shape
    dp_size = lax.axis_size("dp")
    rows_size = lax.axis_size("rows")
    images = img_dev * dp_size
    groups = images // 4
    pixels = rows_dev * rows_size * cols
    count = 4.0 * pixels
    start = lax.axis_index("dp") * img_dev
    labels = jnp.arange(groups, dtype=jnp.int32)
    all_hot = (ghost_group_index[:, None] == labels[None, :]).astype(jnp.float32)
    own_hot = lax.dynamic_slice_in_dim(all_hot, start, img_dev, 0)
    first_kernel, second_kernel, third_kernel = (
        lax.all_gather(first_atrous_weight, "dp", axis=2, tiled=True),
        lax.all_gather(second_atrous_weight, "dp", axis=2, tiled=True),
        lax.all_gather(third_atrous_weight, "dp", axis=2, tiled=True),
    )
    pointwise_output = jnp.einsum(
        "irwc,co->irwo", features, pointwise_weight, preferred_element_type=jnp.float32
    )
    pre = jnp.concatenate(
        [
            pointwise_output,
            dilated_result(features, first_kernel, DILATION_FIRST),
            dilated_result(features, second_kernel, DILATION_SECOND),
            dilated_result(features, third_kernel, DILATION_THIRD),
        ],
        -1,
    )
    group_first, group_second = stats_terms(pre, own_hot)
    pool_part = jnp.sum(features, axis=(1, 2), dtype=jnp.float32)
    pool_total = lax.psum(pool_part, "rows")
    total_first, total_second = lax.psum((group_first, group_second), ("dp", "rows"))
    branches = apply_norm(
        pre,
        own_hot,
        total_first,
        total_second,
        count,
        branch_norm_gain.reshape(-1),
        branch_norm_shift.reshape(-1),
    )
    pooled = (pool_total / pixels).astype(jnp.bfloat16)
    pool_act = jax.nn.relu(
        jnp.dot(pooled, pooling_weight, preferred_element_type=jnp.float32)
    ).astype(jnp.bfloat16)
    pool_map = jnp.broadcast_to(
        pool_act[:, None, None, :], (img_dev, rows_dev, cols, pool_act.shape[1])
    )
    joined = jnp.concatenate([branches, pool_map], -1)
    local_out = project(
        joined, own_hot, projection_weight, count, projection_norm_gain, projection_norm_shift
    )
    return lax.all_to_all(local_out, "dp", split_axis=2, concat_axis=0, tiled=True)


def solution(mesh):
    in_specs = (
        P("dp", "rows", None, None),
        P(None, None, "dp", None),
        P(None, None, "dp", None),
        P(None, None, "dp", None),
        P(),
        P(),
        P(),
        P(),
        P(),
        P(),
        P(),
        P(),
    )
    out_specs = P(None, "rows", "dp", None)
    return jax.shard_map(shards, mesh=mesh, in_specs=in_specs, out_specs=out_specs, check_vma=False)
```

profile of v0, /device:TPU:0, one launch (start us, length us, event | category | flops | bytes accessed | tf_op | source)
XLA Modules:
  0.0 381.6 jit_solution(11481842989761349140)
XLA Ops:
  9.5 1.7 convert_reduce_fusion
  11.2 6.0 %psum.37 = f32[2,1024]{1,0:T(2,128)S(1)} all-reduce(f32[2,1024]{1,0:T(2,128)S(1)} %convert_reduce_fusion), channel_id=1, replica_groups=mesh['dp'=16,'rows'=2] {'rows'}, use_global_device_ids=true, to_apply=%region_5.6 | all-reduce | flops 2048 | bytes 16384 | tf_op jit(solution)/shard_map/psum | solution.py:113
  17.2 1.5 fusion.49
  18.7 46.5 %all-gather.4.cloned.1.call-done = bf16[3,3,1024,256]{3,2,1,0:T(8,128)(2,1)} async-done(((bf16[3,3,64,256]{3,2,1,0:T(8,128)(2,1)}), bf16[3,3,1024,256]{3,2,1,0:T(8,128)(2,1)}) %all-gather.4.cloned.1.call-update) | async-done | bytes 4718608 | tf_op jit(solution)/shard_map/all_gather | solution.py:95
  65.2 2.8 fusion.11
  69.2 1.5 collective-permute-start
  70.7 2.8 fusion.10
  74.7 1.5 collective-permute-start.1
  76.2 42.7 %all-gather.6.cloned.1.call-done = bf16[3,3,1024,256]{3,2,1,0:T(8,128)(2,1)} async-done(((bf16[3,3,64,256]{3,2,1,0:T(8,128)(2,1)}), bf16[3,3,1024,256]{3,2,1,0:T(8,128)(2,1)}) %all-gather.6.cloned.1.call-update) | async-done | bytes 4718608 | tf_op jit(solution)/shard_map/all_gather | solution.py:96
  119.0 2.8 fusion.8
  122.9 1.6 collective-permute-start.2
  124.4 2.8 fusion.7
  128.3 1.5 collective-permute-start.3
  129.9 2.8 fusion.12
  135.1 37.6 %all-gather.8.cloned.1.call-done = bf16[3,3,1024,256]{3,2,1,0:T(8,128)(2,1)} async-done(((bf16[3,3,64,256]{3,2,1,0:T(8,128)(2,1)}), bf16[3,3,1024,256]{3,2,1,0:T(8,128)(2,1)}) %all-gather.8.cloned.1.call-update) | async-done | bytes 4718608 | tf_op jit(solution)/shard_map/all_gather | solution.py:97
  172.7 2.8 fusion.5
  176.8 3.0 fusion.9
  181.2 1.4 fusion.6
  184.1 1.9 fusion.26
  186.0 1.6 fusion.34
  191.9 117.9 %all-reduce.22.cloned.1.call-done = (f32[8,1024]{1,0:T(8,128)}, f32[8,1024]{1,0:T(8,128)}) async-done(((f32[8,1024]{1,0:T(8,128)}, f32[8,1024]{1,0:T(8,128)}), (f32[8,1024]{1,0:T(8,128)}, f32[8,1024]{1,0:T(8,128)})) %all-reduce.22.cloned.1.call-update) | async-done | bytes 65552 | tf_op jit(solution)/shard_map/psum | solution.py:114
  311.7 1.7 maximum_convert_fusion
  314.7 41.1 %all-reduce.18 = (f32[8,256]{1,0:T(8,128)S(1)}, f32[8,256]{1,0:T(8,128)S(1)}) all-reduce(f32[8,256]{1,0:T(8,128)S(1)} %fusion.76, f32[8,256]{1,0:T(8,128)S(1)} %fusion.77), channel_id=1, replica_groups=mesh['dp'=16,'rows'=2] {'dp','rows'}, use_global_device_ids=true, to_apply=%region_9.10 | all-reduce | flops 4096 | bytes 32768 | tf_op jit(solution)/shard_map/psum | solution.py:63
  356.8 17.3 %all_to_all.18 = bf16[2,6,64,256]{3,0,1,2:T(2,128)(2,1)S(1)} all-to-all(bf16[2,6,64,256]{3,0,1,2:T(2,128)(2,1)S(1)} %copy.97), channel_id=1, replica_groups=mesh['dp'=16,'rows'=2] {'dp'}, dimensions={2} | all-to-all | bytes 786432 | tf_op jit(solution)/shard_map/all_to_all | solution.py:135
  (80 shorter events, 23.1 us)
Async XLA Ops:
  6.5 306.9 %copy-start = (bf16[1280,256]{1,0:T(8,128)(2,1)S(1)}, bf16[1280,256]{1,0:T(8,128)(2,1)}, u32[]{:S(2)}) copy-start(bf16[1280,256]{1,0:T(8,128)(2,1)} %param.18) | copy-start | bytes 1966084
  6.5 10.7 %copy-start.2 = (bf16[2,6,64,1024]{3,2,1,0:T(8,128)(2,1)S(1)}, bf16[2,6,64,1024]{3,2,1,0:T(8,128)(2,1)}, u32[]{:S(2)}) copy-start(bf16[2,6,64,1024]{3,2,1,0:T(8,128)(2,1)} %param.12) | copy-start | bytes 4718596
  6.5 10.7 %copy-start.6 = (bf16[1024,256]{1,0:T(8,128)(2,1)S(1)}, bf16[1024,256]{1,0:T(8,128)(2,1)}, u32[]{:S(2)}) copy-start(bf16[1024,256]{1,0:T(8,128)(2,1)} %param.16) | copy-start | bytes 1572868
  6.5 58.7 %all-gather.4.cloned.1.call-start = ((), (), s32[]{:S(2)}) async-start(), calls=%async_computation.1 | async-start | bytes 5013504 | tf_op jit(solution)/shard_map/all_gather | solution.py:95
  7.3 111.7 %all-gather.6.cloned.1.call-start = ((), (), s32[]{:S(2)}) async-start(), calls=%async_computation.2 | async-start | bytes 5013504 | tf_op jit(solution)/shard_map/all_gather | solution.py:96
  8.0 164.7 %all-gather.8.cloned.1.call-start = ((), (), s32[]{:S(2)}) async-start(), calls=%async_computation.3 | async-start | bytes 5013504 | tf_op jit(solution)/shard_map/all_gather | solution.py:97
  8.7 301.0 %all-reduce.22.cloned.1.call-start = ((), (), s32[]{:S(2)}) async-start(), calls=%async_computation.4 | async-start | bytes 131072 | tf_op jit(solution)/shard_map/psum | solution.py:114
  9.5 180.5 %copy-start.10 = (s32[2]{0:T(128)}, s32[2]{0:T(128)S(1)}, u32[]{:S(2)}) copy-start(s32[2]{0:T(128)S(1)} %dynamic-slice) | copy-start | bytes 28
  69.2 113.8 %collective-permute-start = (f32[2,6,64,256]{3,2,1,0:T(8,128)}, f32[2,6,64,256]{3,2,1,0:T(8,128)}, u32[]{:S(2)}, u32[]{:S(2)}) collective-permute-start(f32[2,6,64,256]{3,2,1,0:T(8,128)} %fusion.28), channel_id=1, source_target_pairs={} | collective-permute-start | bytes 2359304 | tf_op jit(solution)/shard_map/ppermute | solution.py:14
  74.7 109.3 %collective-permute-start.1 = (f32[2,6,64,256]{3,2,1,0:T(8,128)}, f32[2,6,64,256]{3,2,1,0:T(8,128)}, u32[]{:S(2)}, u32[]{:S(2)}) collective-permute-start(f32[2,6,64,256]{3,2,1,0:T(8,128)} %fusion.30), channel_id=1, source_target_pairs={} | collective-permute-start | bytes 2359304 | tf_op jit(solution)/shard_map/ppermute | solution.py:14
  122.9 63.2 %collective-permute-start.2 = (f32[2,6,64,256]{3,2,1,0:T(8,128)}, f32[2,6,64,256]{3,2,1,0:T(8,128)}, u32[]{:S(2)}, u32[]{:S(2)}) collective-permute-start(f32[2,6,64,256]{3,2,1,0:T(8,128)} %fusion.36), channel_id=1, source_target_pairs={} | collective-permute-start | bytes 2359304 | tf_op jit(solution)/shard_map/ppermute | solution.py:14
  128.3 57.7 %collective-permute-start.3 = (f32[2,6,64,256]{3,2,1,0:T(8,128)}, f32[2,6,64,256]{3,2,1,0:T(8,128)}, u32[]{:S(2)}, u32[]{:S(2)}) collective-permute-start(f32[2,6,64,256]{3,2,1,0:T(8,128)} %fusion.38), channel_id=1, source_target_pairs={} | collective-permute-start | bytes 2359304 | tf_op jit(solution)/shard_map/ppermute | solution.py:14
  132.7 1.4 copy-start.4
  175.6 4.2 %slice-start = ((s8[4718592]{0:T(1024)(128)(4,1)}), s8[4194304]{0:T(1024)(128)(4,1)S(1)}, s32[]{:S(2)}) async-start(s8[4718592]{0:T(1024)(128)(4,1)} %bitcast.185), calls=%async_computation.5 | async-start | bytes 8388608
  175.7 4.1 %slice-start.1 = ((s8[4718592]{0:T(1024)(128)(4,1)}), s8[524288]{0:T(1024)(128)(4,1)S(1)}, s32[]{:S(2)}) async-start(s8[4718592]{0:T(1024)(128)(4,1)} %bitcast.185), calls=%async_computation.6 | async-start | bytes 1048576
  175.7 11.9 %collective-permute-start.4 = (f32[2,6,64,256]{3,2,1,0:T(8,128)S(1)}, f32[2,6,64,256]{3,2,1,0:T(8,128)S(1)}, u32[]{:S(2)}, u32[]{:S(2)}) collective-permute-start(f32[2,6,64,256]{3,2,1,0:T(8,128)S(1)} %fusion.44), channel_id=1, source_target_pairs={} | collective-permute-start | bytes 2359304 | tf_op jit(solution)/shard_map/ppermute | solution.py:14
  183.0 1.1 copy-start.3
  183.0 4.6 %collective-permute-start.5 = (f32[2,6,64,256]{3,2,1,0:T(8,128)S(1)}, f32[2,6,64,256]{3,2,1,0:T(8,128)S(1)}, u32[]{:S(2)}, u32[]{:S(2)}) collective-permute-start(f32[2,6,64,256]{3,2,1,0:T(8,128)S(1)} %fusion.46), channel_id=1, source_target_pairs={} | collective-permute-start | bytes 2359304 | tf_op jit(solution)/shard_map/ppermute | solution.py:14
  187.7 1.1 copy-start.1
  188.8 2.2 copy-start.5
  188.8 2.4 copy-start.7
  313.5 0.7 copy-start.11
  313.5 42.7 %copy-start.8 = (f32[256]{0:T(256)S(1)}, f32[256]{0:T(256)}, u32[]{:S(2)}) copy-start(f32[256]{0:T(256)} %param.22) | copy-start | bytes 3076
  313.5 42.7 %copy-start.9 = (f32[256]{0:T(256)S(1)}, f32[256]{0:T(256)}, u32[]{:S(2)}) copy-start(f32[256]{0:T(256)} %param.21) | copy-start | bytes 3076
Sparse Core Ops, SparseCore 0:
  9.5 55.6 all-gather.3
  67.4 51.4 all-gather.5
  121.1 51.4 all-gather.7
  191.1 118.6 all-reduce.21
where the time goes:
time: 382 us
  waiting for transfers between devices  247 us (65%)
  blocking collectives  64.4 us (17%)
  matrix products  29.5 us (8%)
  between operations  13.5 us (4%)
  other arithmetic  12 us (3%)
  starting transfers between devices  8.15 us (2%)
  local copies, waits for them, and re-layouts  7.13 us (2%)
    psum x1, waiting for transfers between devices, shards(): lax.psum((group_first, group_second), ('dp', 'rows'))  118 us
    all_gather x1, waiting for transfers between devices, shards(): lax.all_gather(first_atrous_weight, 'dp', axis=2, tiled=True)  46.5 us
    all_gather x1, waiting for transfers between devices, shards(): lax.all_gather(second_atrous_weight, 'dp', axis=2, tiled=True)  42.7 us
    psum x1, blocking collectives, project(): lax.psum((group_first, group_second), ('dp', 'rows'))  41.1 us
    all_gather x1, waiting for transfers between devices, shards(): lax.all_gather(third_atrous_weight, 'dp', axis=2, tiled=True)  37.6 us
    dot_general x9, matrix products, row_tap_list(): jnp.einsum('irwc,kco->irwko', block_tensor, kernel_row_slice, preferred_e...  22.5 us
    all_to_all x1, blocking collectives, shards(): lax.all_to_all(local_out, 'dp', split_axis=2, concat_axis=0, tiled=True)  17.3 us
    ppermute x6, starting transfers between devices, from_behind(): return lax.ppermute(array, axis, pairs)  8.03 us
  transfers between devices with their start and end apart: 10, of which 4 were waited for; matrix products, arithmetic and copies ran while one was open for 10% of the time, Pallas kernels for 0%

commit v1 on v0

--- a/solution.py
+++ b/solution.py
@@ -6,6 +6,12 @@
 DILATION_FIRST = 12
 DILATION_SECOND = 24
 DILATION_THIRD = 36
+
+
+def turn_node(s0, on_dim):
+    kept_arr = list(s0.shape[1:])
+    kept_arr[on_dim] *= s0.shape[0]
+    return jnp.moveaxis(s0, 0, on_dim).reshape(kept_arr)
 
 
 def from_behind(array, axis, by):
@@ -91,9 +97,37 @@
     labels = jnp.arange(groups, dtype=jnp.int32)
     all_hot = (ghost_group_index[:, None] == labels[None, :]).astype(jnp.float32)
     own_hot = lax.dynamic_slice_in_dim(all_hot, start, img_dev, 0)
+
+    def drive_grid_on(tile_in, comm_axis, dim_at):
+        n_parts = lax.psum(1, axis_name=comm_axis)
+        so_far_all = [(ii, (ii + 1) % n_parts) for ii in range(n_parts)]
+        pile = [(tick, it) for it, tick in so_far_all]
+        local_part, raw_out = ([], [])
+        u = 0
+        while u < n_parts - 1:
+            if u % 2 == 0:
+                local_part.append(
+                    lax.ppermute(
+                        local_part[-1] if local_part else tile_in,
+                        axis_name=comm_axis,
+                        perm=so_far_all,
+                    )
+                )
+            else:
+                raw_out.append(
+                    lax.ppermute(
+                        raw_out[-1] if raw_out else tile_in, axis_name=comm_axis, perm=pile
+                    )
+                )
+            u = u + 1
+        field_out = jnp.stack([*local_part[::-1], tile_in, *raw_out])
+        fresh = lax.axis_index(comm_axis) - len(local_part)
+        field_out = field_out[(jnp.arange(n_parts) - fresh) % n_parts]
+        return turn_node(field_out, dim_at)
+
     first_kernel, second_kernel, third_kernel = (
         lax.all_gather(first_atrous_weight, "dp", axis=2, tiled=True),
-        lax.all_gather(second_atrous_weight, "dp", axis=2, tiled=True),
+        drive_grid_on(second_atrous_weight, "dp", 2),
         lax.all_gather(third_atrous_weight, "dp", axis=2, tiled=True),
     )
     pointwise_output = jnp.einsum(

time: 382 us -> 354 us (0.927)
  waiting for transfers between devices: 247 us -> 167 us
  starting transfers between devices: 8.15 us -> 39.3 us
  local copies, waits for them, and re-layouts: 7.13 us -> 32.4 us
    ppermute x0 -> x15, waiting for transfers between devices: none -> 49.3 us  [the longest x8 35.6 us: drive_grid_on(): lax.ppermute(local_part[-1] if local_part else tile_in, axis_name=comm_ax...]
    all_gather x1, waiting for transfers between devices: 46.5 us -> 0.02 us  [shards(): lax.all_gather(first_atrous_weight, 'dp', axis=2, tiled=True)]
    all_gather x1 -> x0, waiting for transfers between devices: 42.7 us -> none  [shards(): lax.all_gather(second_atrous_weight, 'dp', axis=2, tiled=True)]
    all_gather x1, waiting for transfers between devices: 37.6 us -> 0.01 us  [shards(): lax.all_gather(third_atrous_weight, 'dp', axis=2, tiled=True)]
    ppermute x0 -> x15, starting transfers between devices: none -> 32.4 us  [the longest x7 31.8 us: drive_grid_on(): lax.ppermute(raw_out[-1] if raw_out else tile_in, axis_name=comm_axis, pe...]
    unnamed x30 -> x49, local copies, waits for them, and re-layouts: 3.15 us -> 19.5 us
    gather x0 -> x1, local copies, waits for them, and re-layouts: none -> 5.32 us  [drive_grid_on(): field_out = field_out[(jnp.arange(n_parts) - fresh) % n_parts]]
    dot_general x9, matrix products: 22.5 us -> 18.3 us  [row_tap_list(): jnp.einsum('irwc,kco->irwko', block_tensor, kernel_row_slice, preferred_e...]
  transfers between devices with their start and end apart: 10 -> 24, of which waited for: 4 -> 13; matrix products, arithmetic and copies ran while one was open for 10% -> 16% of each run, Pallas kernels for 0% -> 0%
where the time goes in v1:
time: 354 us; the launch traced here: 353 us
  waiting for transfers between devices  167 us (47%)
  blocking collectives  63.4 us (18%)
  starting transfers between devices  39.3 us (11%)
  local copies, waits for them, and re-layouts  32.4 us (9%)
  matrix products  26.8 us (8%)
  between operations  13.6 us (4%)
  other arithmetic  10.5 us (3%)
    psum x1, waiting for transfers between devices, shards(): lax.psum((group_first, group_second), ('dp', 'rows'))  117 us
    psum x1, blocking collectives, project(): lax.psum((group_first, group_second), ('dp', 'rows'))  41.1 us
    ppermute x8, waiting for transfers between devices, drive_grid_on(): lax.ppermute(local_part[-1] if local_part else tile_in, axis_name=comm_ax...  35.6 us
    ppermute x7, starting transfers between devices, drive_grid_on(): lax.ppermute(raw_out[-1] if raw_out else tile_in, axis_name=comm_axis, pe...  31.8 us
    unnamed x49, local copies, waits for them, and re-layouts  19.5 us
    dot_general x9, matrix products, row_tap_list(): jnp.einsum('irwc,kco->irwko', block_tensor, kernel_row_slice, preferred_e...  18.3 us
    all_to_all x1, blocking collectives, shards(): lax.all_to_all(local_out, 'dp', split_axis=2, concat_axis=0, tiled=True)  17.3 us
    ppermute x7, waiting for transfers between devices, drive_grid_on(): lax.ppermute(raw_out[-1] if raw_out else tile_in, axis_name=comm_axis, pe...  13.7 us
  transfers between devices with their start and end apart: 24, of which 13 were waited for; matrix products, arithmetic and copies ran while one was open for 16% of the time, Pallas kernels for 0%

profile of v1, /device:TPU:0, one launch (start us, length us, event | category | flops | bytes accessed | tf_op | source)
XLA Modules:
  0.0 352.7 jit_solution(4148611944452152799)
XLA Ops:
  7.8 9.6 %collective-permute-done.2 = bf16[3,3,64,256]{3,2,1,0:T(8,128)(2,1)S(1)} collective-permute-done((bf16[3,3,64,256]{3,2,1,0:T(8,128)(2,1)}, bf16[3,3,64,256]{3,2,1,0:T(8,128)(2,1)S(1)}, u32[]{:S(2)}, u32[]{:S(2)}) %collective-permute-start.2) | collective-permute-done | bytes 294944 | tf_op jit(solution)/shard_map/ppermute | solution.py:110
  17.4 4.4 %collective-permute-start.10 = (bf16[3,3,64,256]{3,2,1,0:T(8,128)(2,1)}, bf16[3,3,64,256]{3,2,1,0:T(8,128)(2,1)S(1)}, u32[]{:S(2)}, u32[]{:S(2)}) collective-permute-start(bf16[3,3,64,256]{3,2,1,0:T(8,128)(2,1)} %param.14), channel_id=1, source_target_pairs={{2,0},{4,2},{6,4},{8,6},{10,8},{12,10},{14,12},{16,14},{18,16},{20... | collective-permute-start | bytes 884744 | tf_op jit(solution)/shard_map/ppermute | solution.py:118
  21.9 5.1 %collective-permute-done.3 = bf16[3,3,64,256]{3,2,1,0:T(8,128)(2,1)S(1)} collective-permute-done((bf16[3,3,64,256]{3,2,1,0:T(8,128)(2,1)S(1)}, bf16[3,3,64,256]{3,2,1,0:T(8,128)(2,1)S(1)}, u32[]{:S(2)}, u32[]{:S(2)}) %collective-permute-start.3) | collective-permute-done | bytes 294944 | tf_op jit(solution)/shard_map/ppermute | solution.py:110
  27.4 4.6 %collective-permute-start.11 = (bf16[3,3,64,256]{3,2,1,0:T(8,128)(2,1)S(1)}, bf16[3,3,64,256]{3,2,1,0:T(8,128)(2,1)S(1)}, u32[]{:S(2)}, u32[]{:S(2)}) collective-permute-start(bf16[3,3,64,256]{3,2,1,0:T(8,128)(2,1)S(1)} %collective-permute-done.10), channel_id=1, source_target_pairs={{2,0},{4,2},{6,4},{8,6},{10,8},{12,10},{14,12},{16,14},{18,16},{20... | collective-permute-start | bytes 884744 | tf_op jit(solution)/shard_map/ppermute | solution.py:118
  32.0 6.4 %collective-permute-done.4 = bf16[3,3,64,256]{3,2,1,0:T(8,128)(2,1)S(1)} collective-permute-done((bf16[3,3,64,256]{3,2,1,0:T(8,128)(2,1)S(1)}, bf16[3,3,64,256]{3,2,1,0:T(8,128)(2,1)S(1)}, u32[]{:S(2)}, u32[]{:S(2)}) %collective-permute-start.4) | collective-permute-done | bytes 294944 | tf_op jit(solution)/shard_map/ppermute | solution.py:110
  38.4 4.4 %collective-permute-start.12 = (bf16[3,3,64,256]{3,2,1,0:T(8,128)(2,1)S(1)}, bf16[3,3,64,256]{3,2,1,0:T(8,128)(2,1)S(1)}, u32[]{:S(2)}, u32[]{:S(2)}) collective-permute-start(bf16[3,3,64,256]{3,2,1,0:T(8,128)(2,1)S(1)} %collective-permute-done.11), channel_id=1, source_target_pairs={{2,0},{4,2},{6,4},{8,6},{10,8},{12,10},{14,12},{16,14},{18,16},{20... | collective-permute-start | bytes 884744 | tf_op jit(solution)/shard_map/ppermute | solution.py:118
  42.8 4.5 %collective-permute-done.5 = bf16[3,3,64,256]{3,2,1,0:T(8,128)(2,1)S(1)} collective-permute-done((bf16[3,3,64,256]{3,2,1,0:T(8,128)(2,1)S(1)}, bf16[3,3,64,256]{3,2,1,0:T(8,128)(2,1)S(1)}, u32[]{:S(2)}, u32[]{:S(2)}) %collective-permute-start.5) | collective-permute-done | bytes 294944 | tf_op jit(solution)/shard_map/ppermute | solution.py:110
  47.3 5.9 %collective-permute-done.12 = bf16[3,3,64,256]{3,2,1,0:T(8,128)(2,1)S(1)} collective-permute-done((bf16[3,3,64,256]{3,2,1,0:T(8,128)(2,1)S(1)}, bf16[3,3,64,256]{3,2,1,0:T(8,128)(2,1)S(1)}, u32[]{:S(2)}, u32[]{:S(2)}) %collective-permute-start.12) | collective-permute-done | bytes 294944 | tf_op jit(solution)/shard_map/ppermute | solution.py:118
  53.2 4.6 %collective-permute-start.13 = (bf16[3,3,64,256]{3,2,1,0:T(8,128)(2,1)S(1)}, bf16[3,3,64,256]{3,2,1,0:T(8,128)(2,1)S(1)}, u32[]{:S(2)}, u32[]{:S(2)}) collective-permute-start(bf16[3,3,64,256]{3,2,1,0:T(8,128)(2,1)S(1)} %collective-permute-done.12), channel_id=1, source_target_pairs={{2,0},{4,2},{6,4},{8,6},{10,8},{12,10},{14,12},{16,14},{18,16},{20... | collective-permute-start | bytes 884744 | tf_op jit(solution)/shard_map/ppermute | solution.py:118
  57.8 3.4 collective-permute-done.6
  63.7 4.7 %collective-permute-start.14 = (bf16[3,3,64,256]{3,2,1,0:T(8,128)(2,1)S(1)}, bf16[3,3,64,256]{3,2,1,0:T(8,128)(2,1)S(1)}, u32[]{:S(2)}, u32[]{:S(2)}) collective-permute-start(bf16[3,3,64,256]{3,2,1,0:T(8,128)(2,1)S(1)} %collective-permute-done.13), channel_id=1, source_target_pairs={{2,0},{4,2},{6,4},{8,6},{10,8},{12,10},{14,12},{16,14},{18,16},{20... | collective-permute-start | bytes 884744 | tf_op jit(solution)/shard_map/ppermute | solution.py:118
  68.4 3.4 collective-permute-done.7
  72.7 4.9 %collective-permute-done.14 = bf16[3,3,64,256]{3,2,1,0:T(8,128)(2,1)S(1)} collective-permute-done((bf16[3,3,64,256]{3,2,1,0:T(8,128)(2,1)S(1)}, bf16[3,3,64,256]{3,2,1,0:T(8,128)(2,1)S(1)}, u32[]{:S(2)}, u32[]{:S(2)}) %collective-permute-start.14) | collective-permute-done | bytes 294944 | tf_op jit(solution)/shard_map/ppermute | solution.py:118
  77.6 4.6 %collective-permute-start.15 = (bf16[3,3,64,256]{3,2,1,0:T(8,128)(2,1)S(1)}, bf16[3,3,64,256]{3,2,1,0:T(8,128)(2,1)S(1)}, u32[]{:S(2)}, u32[]{:S(2)}) collective-permute-start(bf16[3,3,64,256]{3,2,1,0:T(8,128)(2,1)S(1)} %collective-permute-done.14), channel_id=1, source_target_pairs={{2,0},{4,2},{6,4},{8,6},{10,8},{12,10},{14,12},{16,14},{18,16},{20... | collective-permute-start | bytes 884744 | tf_op jit(solution)/shard_map/ppermute | solution.py:118
  83.8 3.0 fusion.46
  86.7 4.4 %collective-permute-start.16 = (bf16[3,3,64,256]{3,2,1,0:T(8,128)(2,1)S(1)}, bf16[3,3,64,256]{3,2,1,0:T(8,128)(2,1)S(1)}, u32[]{:S(2)}, u32[]{:S(2)}) collective-permute-start(bf16[3,3,64,256]{3,2,1,0:T(8,128)(2,1)S(1)} %collective-permute-done.15), channel_id=1, source_target_pairs={{2,0},{4,2},{6,4},{8,6},{10,8},{12,10},{14,12},{16,14},{18,16},{20... | collective-permute-start | bytes 884744 | tf_op jit(solution)/shard_map/ppermute | solution.py:118
  106.6 5.3 %gather_fusion = bf16[16,3,3,64,256]{4,3,2,1,0:T(8,128)(2,1)} fusion(bf16[16,3,3,64,256]{4,3,2,1,0:T(8,128)(2,1)} %bitcast_dynamic-update-slice_fusion, s32[1024]{0:T(1024)S(1)} %pad_clamp_fusion), kind=kCustom, calls=%fused_computation | custom fusion | bytes 9437248 | tf_op jit(solution)/shard_map/gather | solution.py:125
  111.9 3.4 fusion.96
  124.5 5.0 %psum.37 = f32[2,1024]{1,0:T(2,128)S(1)} all-reduce(f32[2,1024]{1,0:T(2,128)S(1)} %convert_reduce_fusion), channel_id=1, replica_groups=mesh['dp'=16,'rows'=2] {'rows'}, use_global_device_ids=true, to_apply=%region_5.6 | all-reduce | flops 2048 | bytes 16384 | tf_op jit(solution)/shard_map/psum | solution.py:147
  135.3 2.8 fusion.8
  153.8 2.8 fusion.9
  164.2 116.7 %all-reduce.22.cloned.1.call-done = (f32[8,1024]{1,0:T(8,128)}, f32[8,1024]{1,0:T(8,128)}) async-done(((f32[8,1024]{1,0:T(8,128)}, f32[8,1024]{1,0:T(8,128)}), (f32[8,1024]{1,0:T(8,128)}, f32[8,1024]{1,0:T(8,128)})) %all-reduce.22.cloned.1.call-update) | async-done | bytes 65552 | tf_op jit(solution)/shard_map/psum | solution.py:148
  285.9 41.1 %all-reduce.18 = (f32[8,256]{1,0:T(8,128)S(1)}, f32[8,256]{1,0:T(8,128)S(1)}) all-reduce(f32[8,256]{1,0:T(8,128)S(1)} %fusion.73, f32[8,256]{1,0:T(8,128)S(1)} %fusion.74), channel_id=1, replica_groups=mesh['dp'=16,'rows'=2] {'dp','rows'}, use_global_device_ids=true, to_apply=%region_9.10 | all-reduce | flops 4096 | bytes 32768 | tf_op jit(solution)/shard_map/psum | solution.py:69
  328.0 17.3 %all_to_all.18 = bf16[2,6,64,256]{3,0,1,2:T(2,128)(2,1)S(1)} all-to-all(bf16[2,6,64,256]{3,0,1,2:T(2,128)(2,1)S(1)} %copy.79), channel_id=1, replica_groups=mesh['dp'=16,'rows'=2] {'dp'}, dimensions={2} | all-to-all | bytes 786432 | tf_op jit(solution)/shard_map/all_to_all | solution.py:169
  (133 shorter events, 66.7 us)
Async XLA Ops:
  6.5 128.6 %all-gather.3.cloned.1.call-start = ((), (), s32[]{:S(2)}) async-start(), calls=%async_computation.1 | async-start | bytes 5013504 | tf_op jit(solution)/shard_map/all_gather | solution.py:129
  7.3 139.0 %all-gather.5.cloned.1.call-start = ((), (), s32[]{:S(2)}) async-start(), calls=%async_computation.2 | async-start | bytes 5013504 | tf_op jit(solution)/shard_map/all_gather | solution.py:131
  7.3 10.1 %collective-permute-start.2 = (bf16[3,3,64,256]{3,2,1,0:T(8,128)(2,1)}, bf16[3,3,64,256]{3,2,1,0:T(8,128)(2,1)S(1)}, u32[]{:S(2)}, u32[]{:S(2)}) collective-permute-start(bf16[3,3,64,256]{3,2,1,0:T(8,128)(2,1)} %param.14), channel_id=1, source_target_pairs={{0,2},{2,4},{4,6},{6,8},{8,10},{10,12},{12,14},{14,16},{16,18},{18... | collective-permute-start | bytes 884744 | tf_op jit(solution)/shard_map/ppermute | solution.py:110
  17.4 9.6 %collective-permute-start.3 = (bf16[3,3,64,256]{3,2,1,0:T(8,128)(2,1)S(1)}, bf16[3,3,64,256]{3,2,1,0:T(8,128)(2,1)S(1)}, u32[]{:S(2)}, u32[]{:S(2)}) collective-permute-start(bf16[3,3,64,256]{3,2,1,0:T(8,128)(2,1)S(1)} %collective-permute-done.2), channel_id=1, source_target_pairs={{0,2},{2,4},{4,6},{6,8},{8,10},{10,12},{12,14},{14,16},{16,18},{18... | collective-permute-start | bytes 884744 | tf_op jit(solution)/shard_map/ppermute | solution.py:110
  17.4 10.0 %collective-permute-start.10 = (bf16[3,3,64,256]{3,2,1,0:T(8,128)(2,1)}, bf16[3,3,64,256]{3,2,1,0:T(8,128)(2,1)S(1)}, u32[]{:S(2)}, u32[]{:S(2)}) collective-permute-start(bf16[3,3,64,256]{3,2,1,0:T(8,128)(2,1)} %param.14), channel_id=1, source_target_pairs={{2,0},{4,2},{6,4},{8,6},{10,8},{12,10},{14,12},{16,14},{18,16},{20... | collective-permute-start | bytes 884744 | tf_op jit(solution)/shard_map/ppermute | solution.py:118
  27.0 11.4 %collective-permute-start.4 = (bf16[3,3,64,256]{3,2,1,0:T(8,128)(2,1)S(1)}, bf16[3,3,64,256]{3,2,1,0:T(8,128)(2,1)S(1)}, u32[]{:S(2)}, u32[]{:S(2)}) collective-permute-start(bf16[3,3,64,256]{3,2,1,0:T(8,128)(2,1)S(1)} %collective-permute-done.3), channel_id=1, source_target_pairs={{0,2},{2,4},{4,6},{6,8},{8,10},{10,12},{12,14},{14,16},{16,18},{18... | collective-permute-start | bytes 884744 | tf_op jit(solution)/shard_map/ppermute | solution.py:110
  27.4 11.0 %collective-permute-start.11 = (bf16[3,3,64,256]{3,2,1,0:T(8,128)(2,1)S(1)}, bf16[3,3,64,256]{3,2,1,0:T(8,128)(2,1)S(1)}, u32[]{:S(2)}, u32[]{:S(2)}) collective-permute-start(bf16[3,3,64,256]{3,2,1,0:T(8,128)(2,1)S(1)} %collective-permute-done.10), channel_id=1, source_target_pairs={{2,0},{4,2},{6,4},{8,6},{10,8},{12,10},{14,12},{16,14},{18,16},{20... | collective-permute-start | bytes 884744 | tf_op jit(solution)/shard_map/ppermute | solution.py:118
  38.4 8.9 %collective-permute-start.5 = (bf16[3,3,64,256]{3,2,1,0:T(8,128)(2,1)S(1)}, bf16[3,3,64,256]{3,2,1,0:T(8,128)(2,1)S(1)}, u32[]{:S(2)}, u32[]{:S(2)}) collective-permute-start(bf16[3,3,64,256]{3,2,1,0:T(8,128)(2,1)S(1)} %collective-permute-done.4), channel_id=1, source_target_pairs={{0,2},{2,4},{4,6},{6,8},{8,10},{10,12},{12,14},{14,16},{16,18},{18... | collective-permute-start | bytes 884744 | tf_op jit(solution)/shard_map/ppermute | solution.py:110
  38.4 14.9 %collective-permute-start.12 = (bf16[3,3,64,256]{3,2,1,0:T(8,128)(2,1)S(1)}, bf16[3,3,64,256]{3,2,1,0:T(8,128)(2,1)S(1)}, u32[]{:S(2)}, u32[]{:S(2)}) collective-permute-start(bf16[3,3,64,256]{3,2,1,0:T(8,128)(2,1)S(1)} %collective-permute-done.11), channel_id=1, source_target_pairs={{2,0},{4,2},{6,4},{8,6},{10,8},{12,10},{14,12},{16,14},{18,16},{20... | collective-permute-start | bytes 884744 | tf_op jit(solution)/shard_map/ppermute | solution.py:118
  47.3 14.0 %collective-permute-start.6 = (bf16[3,3,64,256]{3,2,1,0:T(8,128)(2,1)S(1)}, bf16[3,3,64,256]{3,2,1,0:T(8,128)(2,1)S(1)}, u32[]{:S(2)}, u32[]{:S(2)}) collective-permute-start(bf16[3,3,64,256]{3,2,1,0:T(8,128)(2,1)S(1)} %collective-permute-done.5), channel_id=1, source_target_pairs={{0,2},{2,4},{4,6},{6,8},{8,10},{10,12},{12,14},{14,16},{16,18},{18... | collective-permute-start | bytes 884744 | tf_op jit(solution)/shard_map/ppermute | solution.py:110
  53.2 10.5 %collective-permute-start.13 = (bf16[3,3,64,256]{3,2,1,0:T(8,128)(2,1)S(1)}, bf16[3,3,64,256]{3,2,1,0:T(8,128)(2,1)S(1)}, u32[]{:S(2)}, u32[]{:S(2)}) collective-permute-start(bf16[3,3,64,256]{3,2,1,0:T(8,128)(2,1)S(1)} %collective-permute-done.12), channel_id=1, source_target_pairs={{2,0},{4,2},{6,4},{8,6},{10,8},{12,10},{14,12},{16,14},{18,16},{20... | collective-permute-start | bytes 884744 | tf_op jit(solution)/shard_map/ppermute | solution.py:118
  61.3 10.5 %collective-permute-start.7 = (bf16[3,3,64,256]{3,2,1,0:T(8,128)(2,1)S(1)}, bf16[3,3,64,256]{3,2,1,0:T(8,128)(2,1)}, u32[]{:S(2)}, u32[]{:S(2)}) collective-permute-start(bf16[3,3,64,256]{3,2,1,0:T(8,128)(2,1)S(1)} %collective-permute-done.6), channel_id=1, source_target_pairs={{0,2},{2,4},{4,6},{6,8},{8,10},{10,12},{12,14},{14,16},{16,18},{18... | collective-permute-start | bytes 884744 | tf_op jit(solution)/shard_map/ppermute | solution.py:110
  63.7 13.9 %collective-permute-start.14 = (bf16[3,3,64,256]{3,2,1,0:T(8,128)(2,1)S(1)}, bf16[3,3,64,256]{3,2,1,0:T(8,128)(2,1)S(1)}, u32[]{:S(2)}, u32[]{:S(2)}) collective-permute-start(bf16[3,3,64,256]{3,2,1,0:T(8,128)(2,1)S(1)} %collective-permute-done.13), channel_id=1, source_target_pairs={{2,0},{4,2},{6,4},{8,6},{10,8},{12,10},{14,12},{16,14},{18,16},{20... | collective-permute-start | bytes 884744 | tf_op jit(solution)/shard_map/ppermute | solution.py:118
  71.8 12.0 %collective-permute-start.8 = (bf16[3,3,64,256]{3,2,1,0:T(8,128)(2,1)}, bf16[3,3,64,256]{3,2,1,0:T(8,128)(2,1)}, u32[]{:S(2)}, u32[]{:S(2)}) collective-permute-start(bf16[3,3,64,256]{3,2,1,0:T(8,128)(2,1)} %collective-permute-done.7), channel_id=1, source_target_pairs={{0,2},{2,4},{4,6},{6,8},{8,10},{10,12},{12,14},{14,16},{16,18},{18... | collective-permute-start | bytes 884744 | tf_op jit(solution)/shard_map/ppermute | solution.py:110
  71.8 209.1 %all-reduce.22.cloned.1.call-start = ((), (), s32[]{:S(2)}) async-start(), calls=%async_computation.3 | async-start | bytes 131072 | tf_op jit(solution)/shard_map/psum | solution.py:148
  77.6 9.1 %collective-permute-start.15 = (bf16[3,3,64,256]{3,2,1,0:T(8,128)(2,1)S(1)}, bf16[3,3,64,256]{3,2,1,0:T(8,128)(2,1)S(1)}, u32[]{:S(2)}, u32[]{:S(2)}) collective-permute-start(bf16[3,3,64,256]{3,2,1,0:T(8,128)(2,1)S(1)} %collective-permute-done.14), channel_id=1, source_target_pairs={{2,0},{4,2},{6,4},{8,6},{10,8},{12,10},{14,12},{16,14},{18,16},{20... | collective-permute-start | bytes 884744 | tf_op jit(solution)/shard_map/ppermute | solution.py:118
  83.7 9.2 %collective-permute-start.9 = (bf16[3,3,64,256]{3,2,1,0:T(8,128)(2,1)}, bf16[3,3,64,256]{3,2,1,0:T(8,128)(2,1)S(1)}, u32[]{:S(2)}, u32[]{:S(2)}) collective-permute-start(bf16[3,3,64,256]{3,2,1,0:T(8,128)(2,1)} %collective-permute-done.8), channel_id=1, source_target_pairs={{0,2},{2,4},{4,6},{6,8},{8,10},{10,12},{12,14},{14,16},{16,18},{18... | collective-permute-start | bytes 884744 | tf_op jit(solution)/shard_map/ppermute | solution.py:110
  86.7 19.1 %collective-permute-start.16 = (bf16[3,3,64,256]{3,2,1,0:T(8,128)(2,1)S(1)}, bf16[3,3,64,256]{3,2,1,0:T(8,128)(2,1)S(1)}, u32[]{:S(2)}, u32[]{:S(2)}) collective-permute-start(bf16[3,3,64,256]{3,2,1,0:T(8,128)(2,1)S(1)} %collective-permute-done.15), channel_id=1, source_target_pairs={{2,0},{4,2},{6,4},{8,6},{10,8},{12,10},{14,12},{16,14},{18,16},{20... | collective-permute-start | bytes 884744 | tf_op jit(solution)/shard_map/ppermute | solution.py:118
  119.3 13.3 %collective-permute-start.17 = (f32[2,6,64,256]{3,2,1,0:T(8,128)}, f32[2,6,64,256]{3,2,1,0:T(8,128)S(1)}, u32[]{:S(2)}, u32[]{:S(2)}) collective-permute-start(f32[2,6,64,256]{3,2,1,0:T(8,128)} %fusion.33), channel_id=1, source_target_pairs={} | collective-permute-start | bytes 2359304 | tf_op jit(solution)/shard_map/ppermute | solution.py:20
  122.7 9.9 %collective-permute-start.18 = (f32[2,6,64,256]{3,2,1,0:T(8,128)}, f32[2,6,64,256]{3,2,1,0:T(8,128)}, u32[]{:S(2)}, u32[]{:S(2)}) collective-permute-start(f32[2,6,64,256]{3,2,1,0:T(8,128)} %fusion.35), channel_id=1, source_target_pairs={} | collective-permute-start | bytes 2359304 | tf_op jit(solution)/shard_map/ppermute | solution.py:20
  139.2 19.1 %collective-permute-start = (f32[2,6,64,256]{3,2,1,0:T(8,128)}, f32[2,6,64,256]{3,2,1,0:T(8,128)}, u32[]{:S(2)}, u32[]{:S(2)}) collective-permute-start(f32[2,6,64,256]{3,2,1,0:T(8,128)} %fusion.25), channel_id=1, source_target_pairs={} | collective-permute-start | bytes 2359304 | tf_op jit(solution)/shard_map/ppermute | solution.py:20
  144.8 13.5 %collective-permute-start.1 = (f32[2,6,64,256]{3,2,1,0:T(8,128)}, f32[2,6,64,256]{3,2,1,0:T(8,128)}, u32[]{:S(2)}, u32[]{:S(2)}) collective-permute-start(f32[2,6,64,256]{3,2,1,0:T(8,128)} %fusion.27), channel_id=1, source_target_pairs={} | collective-permute-start | bytes 2359304 | tf_op jit(solution)/shard_map/ppermute | solution.py:20
  149.4 10.6 %collective-permute-start.19 = (f32[2,6,64,256]{3,2,1,0:T(8,128)S(1)}, f32[2,6,64,256]{3,2,1,0:T(8,128)S(1)}, u32[]{:S(2)}, u32[]{:S(2)}) collective-permute-start(f32[2,6,64,256]{3,2,1,0:T(8,128)S(1)} %fusion.41), channel_id=1, source_target_pairs={} | collective-permute-start | bytes 2359304 | tf_op jit(solution)/shard_map/ppermute | solution.py:20
  153.1 6.9 %collective-permute-start.20 = (f32[2,6,64,256]{3,2,1,0:T(8,128)S(1)}, f32[2,6,64,256]{3,2,1,0:T(8,128)S(1)}, u32[]{:S(2)}, u32[]{:S(2)}) collective-permute-start(f32[2,6,64,256]{3,2,1,0:T(8,128)S(1)} %fusion.43), channel_id=1, source_target_pairs={} | collective-permute-start | bytes 2359304 | tf_op jit(solution)/shard_map/ppermute | solution.py:20
  (16 other events, 509.2 us)
Sparse Core Ops, SparseCore 0:
  9.5 72.7 all-gather.2
  84.5 54.8 all-gather.4
  163.4 117.4 all-reduce.21
